TPU v7x, 128 devices: a whole 4x4x4 slice. The times are simulated.
128 devices in a mesh: seq: 16 (over z_lo, y, core), head: 8 (over z_hi, x).
Axes of the slice: x: 4, y: 4, z: 4 (z_hi: 2, z_lo: 2; z = z_hi * 2 + z_lo), core: 2. Of those that a mesh axis runs over, the one named last changes fastest.
Arguments:
- queries: bfloat16 [8192, 4096], P('seq', 'head'), may hold values from -6 to 6
- new_keys: bfloat16 [8192, 4096], P('seq', 'head'), may hold values from -6 to 6
- new_values: bfloat16 [8192, 4096], P('seq', 'head'), may hold values from -6 to 6
- pool_keys: bfloat16 [16384, 4096], P('seq', 'head'), may hold values from -6 to 6
- pool_values: bfloat16 [16384, 4096], P('seq', 'head'), may hold values from -6 to 6
- cache_len: int32 [4], replicated, may hold values from 128 to 4096, as said below
- cached_table: int32 [4, 32], replicated, may hold values from -1 to 127, as said below
- free_blocks: int32 [4, 16], replicated, may hold values from 0 to 127, as said below
- residual_in: bfloat16 [8192, 7168], P('seq', 'head'), may hold values from -26 to 26
- out_weight: bfloat16 [4096, 7168], P('head'), may hold values from -2.390625 to 2.390625
- out_bias: float32 [7168], P('head'), may hold values from -3 to 3
- ln_gain: float32 [7168], P('head'), may hold values from 0.1 to 1.9
- ln_bias: float32 [7168], P('head'), may hold values from -3 to 3
Outputs:
- hidden: bfloat16 [8192, 7168], P('seq', 'head')
- normed: bfloat16 [8192, 7168], P('seq', 'head')
- keys_out: bfloat16 [16384, 4096], P('seq', 'head')
- values_out: bfloat16 [16384, 4096], P('seq', 'head')
Inputs may be any that keep to these rules, and one draw needn't show every extreme that they name: `cache_len`: a multiple of 128; exactly one prompt has 4096 cached positions. `cached_table`: entry [p, j] names the pool block that holds cached positions j * 128 to j * 128 + 127 of prompt p when j < cache_len[p] / 128, and is -1 otherwise; the named blocks are all different and lie anywhere in the pool. `free_blocks`: all different and never named by cached_table; block free_blocks[p, j] lies in the pool rows held by the same index of seq as token row p * 2048 + j * 128, that is free_blocks[p, j] * 128 // 1024 == (p * 2048 + j * 128) // 512.
All inputs are finite; a program needn't handle non-finite values.
Results may differ from a plain program's by a relative error of at most 0.022.
Values may be sent and summed in bfloat16 or wider, within the bound.
No kernel may reach another device: no remote copies, remote signals or barrier semaphores. Data moves between devices by JAX's collectives and lax.ppermute only.
A program may use at most 384 MiB of HBM per device.

v0:
```python
import jax
import jax.numpy as jnp
from jax import lax
from jax.sharding import PartitionSpec as P

D = 7168
HD = 128
NEW_LEN = 2048
BLOCK = 128
NEGATIVE = -1e30


def key_facts(block_count, cached_table, free_blocks, cache_len):
    block_ids = jnp.arange(block_count, dtype=jnp.int32)
    prompt_count, cached_count = cached_table.shape
    fresh_count = free_blocks.shape[1]
    prompt_ids = jnp.arange(prompt_count, dtype=jnp.int32)
    in_cache = cached_table[None, :, :] == block_ids[:, None, None]
    in_fresh = free_blocks[None, :, :] == block_ids[:, None, None]
    owner = jnp.sum(jnp.where(in_cache, prompt_ids[None, :, None] + 1, 0), axis=(1, 2))
    owner = owner + jnp.sum(jnp.where(in_fresh, prompt_ids[None, :, None] + 1, 0), axis=(1, 2)) - 1
    cached_slot = jnp.arange(cached_count, dtype=jnp.int32)
    fresh_slot = (cache_len // BLOCK)[:, None] + jnp.arange(fresh_count, dtype=jnp.int32)[None, :]
    logical = jnp.sum(jnp.where(in_cache, cached_slot[None, None, :], 0), axis=(1, 2))
    logical = logical + jnp.sum(jnp.where(in_fresh, fresh_slot[None, :, :], 0), axis=(1, 2))
    key_owner = jnp.repeat(owner, BLOCK)
    key_place = (logical[:, None] * BLOCK + jnp.arange(BLOCK, dtype=jnp.int32)[None, :]).reshape(-1)
    return (key_owner, key_place)


def query_facts(first_row, row_count, cache_len):
    rows = first_row + jnp.arange(row_count, dtype=jnp.int32)
    owner = rows // NEW_LEN
    place = rows % NEW_LEN
    prompt_ids = jnp.arange(cache_len.shape[0], dtype=jnp.int32)
    limit = (
        jnp.sum(jnp.where(owner[:, None] == prompt_ids[None, :], cache_len[None, :], 0), axis=1)
        + place
    )
    return (owner, limit)


def attend(query_rows, query_owner, query_limit, keys, values, key_owner, key_place):
    row_count = query_rows.shape[0]
    heads_here = query_rows.shape[1] // HD
    key_count = keys.shape[0]
    query_split = query_rows.reshape(row_count, heads_here, HD)
    key_split = keys.reshape(key_count, heads_here, HD)
    value_split = values.reshape(key_count, heads_here, HD)
    visible = (key_owner[None, :] == query_owner[:, None]) & (
        key_place[None, :] <= query_limit[:, None]
    )
    scores = jnp.einsum(
        "rhd,khd->hrk", query_split, key_split, preferred_element_type=jnp.float32
    ) * HD ** (-0.5)
    scores = jnp.where(visible[None, :, :], scores, NEGATIVE)
    peak = jnp.max(scores, axis=2)
    weights = jnp.where(visible[None, :, :], jnp.exp(scores - peak[:, :, None]), 0.0)
    total = jnp.sum(weights, axis=2)
    mixed = jnp.einsum(
        "hrk,khd->rhd",
        weights.astype(jnp.bfloat16),
        value_split,
        preferred_element_type=jnp.float32,
    )
    return (peak.T, total.T, mixed.reshape(row_count, heads_here * HD))


def combine(first, second):
    peak = jnp.maximum(first[0], second[0])
    scale_first = jnp.exp(first[0] - peak)
    scale_second = jnp.exp(second[0] - peak)
    total = second[1] * scale_second
    row_count, heads_here = peak.shape
    mixed = first[2].reshape(row_count, heads_here, HD) * scale_first[:, :, None]
    mixed = second[2].reshape(row_count, heads_here, HD) * scale_second[:, :, None]
    return (peak, total, mixed.reshape(row_count, heads_here * HD))


def shards(
    queries,
    new_keys,
    new_values,
    pool_keys,
    pool_values,
    cache_len,
    cached_table,
    free_blocks,
    residual_in,
    out_weight,
    out_bias,
    ln_gain,
    ln_bias,
):
    token_rows, width = queries.shape
    heads_here = width // HD
    pool_rows = pool_keys.shape[0]
    per_device = pool_rows // BLOCK
    fresh_device = token_rows // BLOCK
    position = lax.axis_index("seq")
    first_row = position * token_rows
    prompt_here = first_row // NEW_LEN
    first_slot = first_row % NEW_LEN // BLOCK
    targets = (
        lax.dynamic_slice(free_blocks, (prompt_here, first_slot), (1, fresh_device))[0]
        - position * per_device
    )
    keys_out = (
        pool_keys.reshape(per_device, BLOCK, width)
        .at[targets]
        .set(new_keys.reshape(fresh_device, BLOCK, width))
        .reshape(pool_rows, width)
    )
    values_out = (
        pool_values.reshape(per_device, BLOCK, width)
        .at[targets]
        .set(new_values.reshape(fresh_device, BLOCK, width))
        .reshape(pool_rows, width)
    )
    own_owner, own_limit = query_facts(first_row, token_rows, cache_len)
    start_state = (
        jnp.full((token_rows, heads_here), NEGATIVE, jnp.float32),
        jnp.zeros((token_rows, heads_here), jnp.float32),
        jnp.zeros((token_rows, width), jnp.float32),
    )
    piece_keys = lax.all_gather(keys_out, "seq", axis=0, tiled=True)
    piece_values = lax.all_gather(values_out, "seq", axis=0, tiled=True)
    key_owner, key_place = key_facts(
        piece_keys.shape[0] // BLOCK, cached_table, free_blocks, cache_len
    )
    peak, total, mixed = combine(
        start_state,
        attend(queries, own_owner, own_limit, piece_keys, piece_values, key_owner, key_place),
    )
    attn = (
        (mixed.reshape(token_rows, heads_here, HD) / total[:, :, None])
        .reshape(token_rows, width)
        .astype(jnp.bfloat16)
    )
    projected = jnp.dot(attn, out_weight, preferred_element_type=jnp.float32)
    summed = lax.psum_scatter(
        projected.astype(jnp.bfloat16), "head", scatter_dimension=1, tiled=True
    ).astype(jnp.float32)
    stream = residual_in.astype(jnp.float32) + summed + out_bias[None, :]
    mean = lax.psum(jnp.sum(stream, axis=1), "head") / D
    centred = stream - mean[:, None]
    variance = lax.psum(jnp.sum(centred * centred, axis=1), "head") / D
    normed = (
        centred * lax.rsqrt(variance[:, None] + 1e-05) * ln_gain[None, :] + ln_bias[None, :]
    ).astype(jnp.bfloat16)
    return (stream.astype(jnp.bfloat16), normed, keys_out, values_out)


def solution(mesh):
    in_specs = (
        P("seq", "head"),
        P("seq", "head"),
        P("seq", "head"),
        P("seq", "head"),
        P("seq", "head"),
        P(),
        P(),
        P(),
        P("seq", "head"),
        P("head", None),
        P("head"),
        P("head"),
        P("head"),
    )
    out_specs = (P("seq", "head"), P("seq", "head"), P("seq", "head"), P("seq", "head"))
    return jax.shard_map(shards, mesh=mesh, in_specs=in_specs, out_specs=out_specs, check_vma=False)
```

profile of v0, /device:TPU:0, one launch (start us, length us, event | category | flops | bytes accessed | tf_op | source)
XLA Modules:
  0.0 465.4 jit_solution(8003422405766926117)
XLA Ops:
  7.2 0.0 copy-start
  7.2 0.0 all-gather.5.cloned.1.call-start
  7.2 1.3 copy.59
  8.5 1.2 copy.60
  9.7 0.8 fusion.22
  10.5 1.7 scatter_fusion.1
  12.2 0.0 copy-start.4
  12.2 1.3 copy.38
  13.5 0.0 all-gather.5.cloned.1.call-update
  13.5 0.0 all-gather.3.cloned.1.call-start
  13.6 1.7 scatter_fusion
  15.3 0.0 copy-start.3
  15.3 1.0 copy-done.3
  16.3 0.0 all-gather.3.cloned.1.call-update
  16.3 0.0 reduce-scatter.4.cloned.1.call-start
  16.4 0.7 select_reduce_fusion.4
  17.1 0.8 select_reduce_fusion.1
  17.9 0.7 and_select_fusion
  18.6 0.1 iota_add_fusion
  18.6 0.8 select_reduce_fusion.3
  19.4 0.1 add_bitcast_fusion
  19.5 0.1 broadcast_bitcast_fusion
  19.6 13.3 %compare_and_fusion = pred[512,16384]{0,1:T(8,128)(4,1)} fusion(s32[512]{0:T(512)S(1)} %fusion.18, s32[512]{0:T(512)S(1)} %add_select_fusion.1, s32[16384]{0:T(1024)S(1)} %add_bitcast_fusion, s32[16384]{0:T(1024)S(1)} %broadcast_bitcast_fusion), kind=kLoop, calls=%fused_computation.9 | loop fusion | flops 25165824 | bytes 8523776 | tf_op jit(solution)/shard_map/and | solution.py:50
  32.9 74.9 %all-gather.5.cloned.1.call-done = bf16[16384,512]{0,1:T(8,128)(2,1)} async-done(((bf16[1024,512]{0,1:T(8,128)(2,1)}), bf16[16384,512]{0,1:T(8,128)(2,1)}) %all-gather.5.cloned.1.call-update) | async-done | bytes 16777232 | tf_op jit(solution)/shard_map/all_gather | solution.py:126
  107.8 0.0 copy-done
  107.8 59.0 %fusion = (f32[4,512]{1,0:T(4,128)S(1)}, f32[4,16384,512]{2,1,0:T(8,128)}) fusion(pred[512,16384]{0,1:T(8,128)(4,1)} %compare_and_fusion, bf16[16384,4,128]{0,2,1:T(8,128)(2,1)} %bitcast.79, bf16[512,512]{1,0:T(8,128)(2,1)S(1)} %copy-done), kind=kOutput, calls=%fused_computation.4 | convolution fusion | flops 8690595840 | bytes 159916032 | tf_op jit(solution)/shard_map/rhd,khd->hrk/dot_general | solution.py:53
  166.8 0.0 copy-done.4
  166.8 45.4 %fusion.1 = f32[4,512]{1,0:T(4,128)S(1)} fusion(f32[4,16384,512]{2,1,0:T(8,128)} %get-tuple-element.17, f32[4,512]{1,0:T(4,128)S(1)} %get-tuple-element.16, pred[512,16384]{0,1:T(8,128)(4,1)} %compare_and_fusion), kind=kLoop, calls=%fused_computation.5 | loop fusion | flops 167770112 | bytes 142622720 | tf_op jit(solution)/shard_map/reduce_sum | solution.py:59
  212.2 0.0 all-gather.3.cloned.1.call-done
  212.2 21.3 %copy.37 = bf16[16384,512]{0,1:T(8,128)(2,1)} copy(bf16[16384,512]{1,0:T(8,128)(2,1)} %all-gather.3.cloned.1.call-done) | data formatting | bytes 33554432 | tf_op jit(solution)/shard_map/all_gather | solution.py:127
  233.5 52.8 %divide_convert_fusion = bf16[512,4,128]{0,2,1:T(8,128)(2,1)S(1)} fusion(f32[512,4]{0,1:T(4,128)S(1)} %get-tuple-element.14, f32[512,4]{0,1:T(4,128)S(1)} %get-tuple-element.15, bf16[16384,4,128]{0,2,1:T(8,128)(2,1)} %bitcast.68, f32[4,16384,512]{2,1,0:T(8,128)} %get-tuple-element.17, f32[4,512]{1,0:T(4,128)S(1)} %get-tuple-element.16, ...), kind=kOutput, calls=%fused_computation.18 | convolution fusion | flops 8758493184 | bytes 159932416 | tf_op jit(solution)/shard_map/hrk,khd->rhd/dot_general | solution.py:60
  286.3 0.0 copy-start.2
  286.3 0.0 copy-start.5
  286.3 0.0 copy-start.1
  286.3 9.5 %convolution_convert_fusion = bf16[512,7168]{1,0:T(8,128)(2,1)} fusion(bf16[512,512]{0,1:T(8,128)(2,1)S(1)} %bitcast.78, bf16[512,7168]{1,0:T(8,128)(2,1)} %param.22), kind=kOutput, calls=%fused_computation.10 | convolution fusion | flops 3761766400 | bytes 15204352 | tf_op jit(solution)/shard_map/dot_general | solution.py:140
  295.9 0.0 copy-start.6
  295.9 0.0 copy-start.7
  295.9 10.4 %copy.44 = bf16[512,7168]{0,1:T(8,128)(2,1)} copy(bf16[512,7168]{1,0:T(8,128)(2,1)} %convolution_convert_fusion) | data formatting | bytes 14680064
  306.3 0.0 reduce-scatter.4.cloned.1.call-update
  306.3 108.4 %reduce-scatter.4.cloned.1.call-done = bf16[896,512]{1,0:T(8,128)(2,1)} async-done(((bf16[7168,512]{1,0:T(8,128)(2,1)}), bf16[896,512]{1,0:T(8,128)(2,1)}) %reduce-scatter.4.cloned.1.call-update) | async-done | bytes 917520
  414.7 1.5 copy.45
  416.3 0.0 copy-done.2
  416.3 0.0 copy-done.5
  416.3 0.4 fusion.12
  416.7 20.3 %psum.14 = f32[512]{0:T(512)S(1)} all-reduce(f32[512]{0:T(512)S(1)} %fusion.12), channel_id=1, replica_groups=mesh['seq'=16,'head'=8] {'head'}, use_global_device_ids=true, to_apply=%region_11.12 | all-reduce | flops 512 | bytes 4096 | tf_op jit(solution)/shard_map/psum | solution.py:145
  437.0 0.5 multiply_reduce_fusion
  437.5 19.6 %psum.15 = f32[512]{0:T(512)S(1)} all-reduce(f32[512]{0:T(512)S(1)} %multiply_reduce_fusion), channel_id=1, replica_groups=mesh['seq'=16,'head'=8] {'head'}, use_global_device_ids=true, to_apply=%region_13.14 | all-reduce | flops 512 | bytes 4096 | tf_op jit(solution)/shard_map/psum | solution.py:147
  457.1 0.0 copy-done.6
  457.1 0.0 copy-done.7
  457.1 1.8 add_convert_fusion
  458.9 0.0 copy-done.1
  (7 shorter events, 0.1 us)
Async XLA Ops:
  7.2 100.6 %copy-start = (bf16[512,512]{1,0:T(8,128)(2,1)S(1)}, bf16[512,512]{1,0:T(8,128)(2,1)}, u32[]{:S(2)}) copy-start(bf16[512,512]{1,0:T(8,128)(2,1)} %param.13) | copy-start | bytes 1572868
  7.2 100.6 %all-gather.5.cloned.1.call-start = ((), (), s32[]{:S(2)}) async-start(), calls=%async_computation.2 | async-start | bytes 17825792 | tf_op jit(solution)/shard_map/all_gather | solution.py:126
  12.2 154.6 %copy-start.4 = (bf16[8,128,512]{2,1,0:T(8,128)(2,1)}, bf16[8,128,512]{2,1,0:T(8,128)(2,1)S(1)}, u32[]{:S(2)}) copy-start(bf16[8,128,512]{2,1,0:T(8,128)(2,1)S(1)} %scatter_fusion.1) | copy-start | bytes 3145732
  13.5 198.6 %all-gather.3.cloned.1.call-start = ((), (), s32[]{:S(2)}) async-start(), calls=%async_computation.1 | async-start | bytes 17825792 | tf_op jit(solution)/shard_map/all_gather | solution.py:127
  15.3 1.0 copy-start.3
  16.3 398.4 %reduce-scatter.4.cloned.1.call-start = ((), (), s32[]{:S(2)}) async-start(), calls=%async_computation.3 | async-start | bytes 8257536
  286.3 130.0 %copy-start.2 = (bf16[512,896]{1,0:T(8,128)(2,1)S(1)}, bf16[512,896]{1,0:T(8,128)(2,1)}, u32[]{:S(2)}) copy-start(bf16[512,896]{1,0:T(8,128)(2,1)} %param.21) | copy-start | bytes 2752516
  286.3 130.0 %copy-start.5 = (f32[896]{0:T(1024)S(1)}, f32[896]{0:T(1024)}, u32[]{:S(2)}) copy-start(f32[896]{0:T(1024)} %param.23) | copy-start | bytes 10756
  286.3 172.6 %copy-start.1 = (bf16[512,512]{1,0:T(8,128)(2,1)S(1)}, bf16[512,512]{1,0:T(8,128)(2,1)}, u32[]{:S(2)}) copy-start(bf16[512,512]{1,0:T(8,128)(2,1)} %param.13) | copy-start | bytes 1572868
  295.9 161.2 %copy-start.6 = (f32[896]{0:T(1024)S(1)}, f32[896]{0:T(1024)}, u32[]{:S(2)}) copy-start(f32[896]{0:T(1024)} %param.25) | copy-start | bytes 10756
  295.9 161.2 %copy-start.7 = (f32[896]{0:T(1024)S(1)}, f32[896]{0:T(1024)}, u32[]{:S(2)}) copy-start(f32[896]{0:T(1024)} %param.24) | copy-start | bytes 10756
Sparse Core Ops, SparseCore 0:
  13.7 94.0 all-gather.4
  110.1 92.4 all-gather.2
  306.5 108.2 reduce-scatter.3
where the time goes:
time: 467 us; the launch traced here: 465 us
  waiting for transfers between devices  183 us (39%)
  matrix products  121 us (26%)
  other arithmetic  65.2 us (14%)
  local copies, waits for them, and re-layouts  41.5 us (9%)
  blocking collectives  39.9 us (9%)
  between operations  13.9 us (3%)
    unnamed x4, waiting for transfers between devices  108 us
    all_gather x1, waiting for transfers between devices, shards(): piece_keys = lax.all_gather(keys_out, 'seq', axis=0, tiled=True)  74.9 us
    dot_general x1, matrix products, attend(): jnp.einsum('rhd,khd->hrk', query_split, key_split, preferred_element_type...  59 us
    dot_general x1, matrix products, attend(): jnp.einsum('hrk,khd->rhd', weights.astype(jnp.bfloat16), value_split, pre...  52.8 us
    reduce_sum x1, other arithmetic, attend(): total = jnp.sum(weights, axis=2)  45.4 us
    all_gather x1, local copies, waits for them, and re-layouts, shards(): piece_values = lax.all_gather(values_out, 'seq', axis=0, tiled=True)  21.3 us
    psum x1, blocking collectives, shards(): mean = lax.psum(jnp.sum(stream, axis=1), 'head') / D  20.3 us
    psum x1, blocking collectives, shards(): variance = lax.psum(jnp.sum(centred * centred, axis=1), 'head') / D  19.6 us
  transfers between devices with their start and end apart: 3, of which 2 were waited for; matrix products, arithmetic and copies ran while one was open for 26% of the time, Pallas kernels for 0%

commit v1 on v0

--- a/solution.py
+++ b/solution.py
@@ -8,6 +8,11 @@
 NEW_LEN = 2048
 BLOCK = 128
 NEGATIVE = -1e30
+tell_cycles = lambda array_in, unit: jnp.split(
+    jax.lax.all_gather(jnp.concatenate([array_in, unit], 1), "seq", axis=0, tiled=True),
+    [array_in.shape[1]],
+    1,
+)
 
 
 def key_facts(block_count, cached_table, free_blocks, cache_len):
@@ -123,8 +128,7 @@
         jnp.zeros((token_rows, heads_here), jnp.float32),
         jnp.zeros((token_rows, width), jnp.float32),
     )
-    piece_keys = lax.all_gather(keys_out, "seq", axis=0, tiled=True)
-    piece_values = lax.all_gather(values_out, "seq", axis=0, tiled=True)
+    piece_keys, piece_values = tell_cycles(keys_out, unit=values_out)
     key_owner, key_place = key_facts(
         piece_keys.shape[0] // BLOCK, cached_table, free_blocks, cache_len
     )

time: 467 us -> 548 us (1.17)
  waiting for transfers between devices: 183 us -> 268 us
    all_gather x2 -> x1, waiting for transfers between devices: 74.9 us -> 159 us  [jax.lax.all_gather(jnp.concatenate([array_in, unit], 1), 'seq', axis=0, t...]
    split x0 -> x1, local copies, waits for them, and re-layouts: none -> 22.8 us  [jnp.split(jax.lax.all_gather(jnp.concatenate([array_in, unit], 1), 'seq',...]
    all_gather x1 -> x0, local copies, waits for them, and re-layouts: 21.3 us -> none  [shards(): piece_values = lax.all_gather(values_out, 'seq', axis=0, tiled=True)]
    unnamed x20 -> x26, local copies, waits for them, and re-layouts: 15.5 us -> 14.6 us
    unnamed x4 -> x3, waiting for transfers between devices: 108 us -> 109 us
  transfers between devices with their start and end apart: 3 -> 2, of which waited for: 2 -> 2; matrix products, arithmetic and copies ran while one was open for 26% -> 3% of each run, Pallas kernels for 0% -> 0%
where the time goes in v1:
time: 548 us
  waiting for transfers between devices  268 us (49%)
  matrix products  118 us (22%)
  other arithmetic  64 us (12%)
  local copies, waits for them, and re-layouts  43.5 us (8%)
  blocking collectives  39.9 us (7%)
  between operations  14.2 us (3%)
    all_gather x1, waiting for transfers between devices, jax.lax.all_gather(jnp.concatenate([array_in, unit], 1), 'seq', axis=0, t...  159 us
    unnamed x3, waiting for transfers between devices  109 us
    dot_general x1, matrix products, attend(): jnp.einsum('rhd,khd->hrk', query_split, key_split, preferred_element_type...  55.8 us
    dot_general x1, matrix products, attend(): jnp.einsum('hrk,khd->rhd', weights.astype(jnp.bfloat16), value_split, pre...  52.8 us
    reduce_sum x1, other arithmetic, attend(): total = jnp.sum(weights, axis=2)  43.7 us
    split x1, local copies, waits for them, and re-layouts, jnp.split(jax.lax.all_gather(jnp.concatenate([array_in, unit], 1), 'seq',...  22.8 us
    psum x1, blocking collectives, shards(): mean = lax.psum(jnp.sum(stream, axis=1), 'head') / D  20.3 us
    psum x1, blocking collectives, shards(): variance = lax.psum(jnp.sum(centred * centred, axis=1), 'head') / D  19.6 us
  transfers between devices with their start and end apart: 2, of which 2 were waited for; matrix products, arithmetic and copies ran while one was open for 3% of the time, Pallas kernels for 0%

profile of v1, /device:TPU:0, one launch (start us, length us, event | category | flops | bytes accessed | tf_op | source)
XLA Modules:
  0.0 547.9 jit_solution(17023375459639259488)
XLA Ops:
  7.2 0.0 copy-start
  7.2 0.0 copy-start.10
  7.2 0.0 copy-start.9
  7.2 0.0 copy-start.8
  7.2 0.0 all-gather.2.cloned.1.call-start
  7.3 1.3 copy.61
  8.5 1.2 copy.62
  9.8 0.8 fusion.22
  10.5 1.7 scatter_fusion
  12.2 0.0 copy-start.4
  12.2 1.3 copy.39
  13.6 1.7 scatter_fusion.1
  15.3 0.0 copy-start.3
  15.3 1.3 copy.40
  16.6 3.0 pad_maximum_fusion
  19.6 0.0 all-gather.2.cloned.1.call-update
  19.7 0.0 reduce-scatter.4.cloned.1.call-start
  19.7 0.0 copy-done.10
  19.7 0.1 select_reduce_fusion.4
  19.8 0.0 copy-done.9
  19.8 0.1 select_reduce_fusion.1
  20.0 0.1 iota_add_fusion
  20.0 0.0 copy-done.8
  20.0 0.1 select_reduce_fusion.3
  20.2 0.1 add_bitcast_fusion
  20.2 0.1 broadcast_bitcast_fusion
  20.3 13.3 %compare_and_fusion = pred[512,16384]{0,1:T(8,128)(4,1)} fusion(s32[512]{0:T(512)S(1)} %fusion.18, s32[512]{0:T(512)S(1)} %add_select_fusion.1, s32[16384]{0:T(1024)S(1)} %add_bitcast_fusion, s32[16384]{0:T(1024)S(1)} %broadcast_bitcast_fusion), kind=kLoop, calls=%fused_computation.9 | loop fusion | flops 25165824 | bytes 8523776 | tf_op jit(solution)/shard_map/and | solution.py:55
  33.6 159.3 %all-gather.2.cloned.1.call-done = bf16[16384,1024]{0,1:T(8,128)(2,1)} async-done(((bf16[1024,1024]{0,1:T(8,128)(2,1)}), bf16[16384,1024]{0,1:T(8,128)(2,1)}) %all-gather.2.cloned.1.call-update) | async-done | bytes 33554448 | tf_op jit(solution)/shard_map/all_gather | solution.py:12
  192.9 22.8 %fusion.26 = (bf16[16384,512]{0,1:T(8,128)(2,1)}, bf16[16384,512]{0,1:T(8,128)(2,1)}) fusion(bf16[16384,1024]{0,1:T(8,128)(2,1)} %all-gather.2.cloned.1.call-done), kind=kLoop, calls=%fused_computation.62 | loop fusion | bytes 67108864 | tf_op jit(solution)/shard_map/split | solution.py:11
  215.7 0.0 copy-done.4
  215.8 0.0 copy-done.3
  215.8 0.0 copy-done
  215.8 55.8 %fusion = (f32[4,512]{1,0:T(4,128)S(1)}, f32[4,16384,512]{2,1,0:T(8,128)}) fusion(pred[512,16384]{0,1:T(8,128)(4,1)} %compare_and_fusion, bf16[16384,4,128]{0,2,1:T(8,128)(2,1)} %bitcast.69, bf16[512,512]{1,0:T(8,128)(2,1)S(1)} %copy-done), kind=kOutput, calls=%fused_computation.4 | convolution fusion | flops 8690595840 | bytes 159916032 | tf_op jit(solution)/shard_map/rhd,khd->hrk/dot_general | solution.py:58
  271.6 43.7 %fusion.1 = f32[4,512]{1,0:T(4,128)S(1)} fusion(f32[4,16384,512]{2,1,0:T(8,128)} %get-tuple-element.19, f32[4,512]{1,0:T(4,128)S(1)} %get-tuple-element.18, pred[512,16384]{0,1:T(8,128)(4,1)} %compare_and_fusion), kind=kLoop, calls=%fused_computation.5 | loop fusion | flops 167770112 | bytes 142622720 | tf_op jit(solution)/shard_map/reduce_sum | solution.py:64
  315.3 52.8 %divide_convert_fusion = bf16[512,4,128]{0,2,1:T(8,128)(2,1)S(1)} fusion(f32[512,4]{0,1:T(4,128)S(1)} %get-tuple-element.16, f32[512,4]{0,1:T(4,128)S(1)} %get-tuple-element.17, bf16[16384,4,128]{0,2,1:T(8,128)(2,1)} %bitcast.68, f32[4,16384,512]{2,1,0:T(8,128)} %get-tuple-element.19, f32[4,512]{1,0:T(4,128)S(1)} %get-tuple-element.18, ...), kind=kOutput, calls=%fused_computation.19 | convolution fusion | flops 8758493184 | bytes 159932416 | tf_op jit(solution)/shard_map/hrk,khd->rhd/dot_general | solution.py:65
  368.2 0.0 copy-start.1
  368.2 9.4 %convolution_convert_fusion = bf16[512,7168]{1,0:T(8,128)(2,1)} fusion(bf16[512,512]{0,1:T(8,128)(2,1)S(1)} %bitcast.79, bf16[512,7168]{1,0:T(8,128)(2,1)} %param.22), kind=kOutput, calls=%fused_computation.10 | convolution fusion | flops 3761766400 | bytes 15204352 | tf_op jit(solution)/shard_map/dot_general | solution.py:144
  377.6 0.0 copy-start.2
  377.6 0.0 copy-start.5
  377.6 0.0 copy-start.6
  377.6 0.0 copy-start.7
  377.6 10.5 %copy.46 = bf16[512,7168]{0,1:T(8,128)(2,1)} copy(bf16[512,7168]{1,0:T(8,128)(2,1)} %convolution_convert_fusion) | data formatting | bytes 14680064
  388.1 0.0 reduce-scatter.4.cloned.1.call-update
  388.1 108.7 %reduce-scatter.4.cloned.1.call-done = bf16[896,512]{1,0:T(8,128)(2,1)} async-done(((bf16[7168,512]{1,0:T(8,128)(2,1)}), bf16[896,512]{1,0:T(8,128)(2,1)}) %reduce-scatter.4.cloned.1.call-update) | async-done | bytes 917520
  496.9 1.5 copy.47
  498.4 0.0 copy-done.2
  498.4 0.0 copy-done.5
  498.4 0.4 fusion.12
  498.8 20.3 %psum.14 = f32[512]{0:T(512)S(1)} all-reduce(f32[512]{0:T(512)S(1)} %fusion.12), channel_id=1, replica_groups=mesh['seq'=16,'head'=8] {'head'}, use_global_device_ids=true, to_apply=%region_11.12 | all-reduce | flops 512 | bytes 4096 | tf_op jit(solution)/shard_map/psum | solution.py:149
  519.1 0.5 multiply_reduce_fusion
  519.7 19.6 %psum.15 = f32[512]{0:T(512)S(1)} all-reduce(f32[512]{0:T(512)S(1)} %multiply_reduce_fusion), channel_id=1, replica_groups=mesh['seq'=16,'head'=8] {'head'}, use_global_device_ids=true, to_apply=%region_13.14 | all-reduce | flops 512 | bytes 4096 | tf_op jit(solution)/shard_map/psum | solution.py:151
  539.2 0.0 copy-done.6
  539.2 0.0 copy-done.7
  539.2 1.8 add_convert_fusion
  541.0 0.0 copy-done.1
  (8 shorter events, 0.1 us)
Async XLA Ops:
  7.2 208.6 %copy-start = (bf16[512,512]{1,0:T(8,128)(2,1)S(1)}, bf16[512,512]{1,0:T(8,128)(2,1)}, u32[]{:S(2)}) copy-start(bf16[512,512]{1,0:T(8,128)(2,1)} %param.13) | copy-start | bytes 1572868
  7.2 12.6 %copy-start.10 = (s32[4]{0:T(128)S(1)}, s32[4]{0:T(128)}, u32[]{:S(2)}) copy-start(s32[4]{0:T(128)} %param.18) | copy-start | bytes 52
  7.2 12.6 %copy-start.9 = (s32[4,32]{1,0:T(4,128)S(1)}, s32[4,32]{1,0:T(4,128)}, u32[]{:S(2)}) copy-start(s32[4,32]{1,0:T(4,128)} %param.19) | copy-start | bytes 1540
  7.2 12.8 %copy-start.8 = (s32[4,16]{1,0:T(4,128)S(1)}, s32[4,16]{1,0:T(4,128)}, u32[]{:S(2)}) copy-start(s32[4,16]{1,0:T(4,128)} %param.20) | copy-start | bytes 772
  7.2 185.7 %all-gather.2.cloned.1.call-start = ((), (), s32[]{:S(2)}) async-start(), calls=%async_computation.1 | async-start | bytes 35651584 | tf_op jit(solution)/shard_map/all_gather | solution.py:12
  12.2 203.5 %copy-start.4 = (bf16[8,128,512]{2,1,0:T(8,128)(2,1)}, bf16[8,128,512]{2,1,0:T(8,128)(2,1)S(1)}, u32[]{:S(2)}) copy-start(bf16[8,128,512]{2,1,0:T(8,128)(2,1)S(1)} %scatter_fusion) | copy-start | bytes 3145732
  15.3 200.5 %copy-start.3 = (bf16[8,128,512]{2,1,0:T(8,128)(2,1)}, bf16[8,128,512]{2,1,0:T(8,128)(2,1)S(1)}, u32[]{:S(2)}) copy-start(bf16[8,128,512]{2,1,0:T(8,128)(2,1)S(1)} %scatter_fusion.1) | copy-start | bytes 3145732
  19.7 477.2 %reduce-scatter.4.cloned.1.call-start = ((), (), s32[]{:S(2)}) async-start(), calls=%async_computation.2 | async-start | bytes 8257536
  368.2 172.9 %copy-start.1 = (bf16[512,512]{1,0:T(8,128)(2,1)S(1)}, bf16[512,512]{1,0:T(8,128)(2,1)}, u32[]{:S(2)}) copy-start(bf16[512,512]{1,0:T(8,128)(2,1)} %param.13) | copy-start | bytes 1572868
  377.6 120.8 %copy-start.2 = (bf16[512,896]{1,0:T(8,128)(2,1)S(1)}, bf16[512,896]{1,0:T(8,128)(2,1)}, u32[]{:S(2)}) copy-start(bf16[512,896]{1,0:T(8,128)(2,1)} %param.21) | copy-start | bytes 2752516
  377.6 120.8 %copy-start.5 = (f32[896]{0:T(1024)S(1)}, f32[896]{0:T(1024)}, u32[]{:S(2)}) copy-start(f32[896]{0:T(1024)} %param.23) | copy-start | bytes 10756
  377.6 161.6 %copy-start.6 = (f32[896]{0:T(1024)S(1)}, f32[896]{0:T(1024)}, u32[]{:S(2)}) copy-start(f32[896]{0:T(1024)} %param.25) | copy-start | bytes 10756
  377.6 161.6 %copy-start.7 = (f32[896]{0:T(1024)S(1)}, f32[896]{0:T(1024)}, u32[]{:S(2)}) copy-start(f32[896]{0:T(1024)} %param.24) | copy-start | bytes 10756
Sparse Core Ops, SparseCore 0:
  19.8 173.1 all-gather.1
  388.3 108.5 reduce-scatter.3
